TPU v7x, 256 devices: a whole 4x4x8 slice. The times are simulated.
256 devices in a mesh: clip: 16 (over y_lo, z), chan: 16 (over x, y_hi, core).
Axes of the slice: x: 4, y: 4 (y_hi: 2, y_lo: 2; y = y_hi * 2 + y_lo), z: 8, core: 2. Of those that a mesh axis runs over, the one named last changes fastest.
Arguments:
- block_in: bfloat16 [16, 512, 4, 4, 128], P('clip', 'chan'), may hold values from -6 to 6
- conv_one: bfloat16 [512, 27, 512], P('chan'), may hold values from -0.0546875 to 0.0546875
- conv_two: bfloat16 [512, 27, 512], P('chan'), may hold values from -0.0546875 to 0.0546875
- out_cotangent: bfloat16 [16, 512, 4, 4, 128], P('clip', 'chan'), may hold values from -6 to 6
Outputs:
- block_out: float32 [16, 512, 4, 4, 128], P('clip', 'chan')
- block_in_grad: float32 [16, 512, 4, 4, 128], P('clip', 'chan')
- conv_one_grad: float32 [512, 27, 512], P('chan')
- conv_two_grad: float32 [512, 27, 512], P('chan')
All inputs are finite; a program needn't handle non-finite values.
Results may differ from a plain program's by a relative error of at most 0.0046.
Values may be sent and summed in bfloat16 or wider, within the bound.
No kernel may reach another device: no remote copies, remote signals or barrier semaphores. Data moves between devices by JAX's collectives and lax.ppermute only.
A program may use at most 64 MiB of HBM per device.

v0:
```python
import jax
import jax.numpy as jnp
from jax import lax
from jax.sharding import PartitionSpec as P

C = 512
GROUPS = 32


def norm_act(field):
    shape = field.shape
    size = C // GROUPS
    grouped = field.reshape(shape[0] // size, size, -1)
    center = jnp.mean(grouped, axis=(1, 2), keepdims=True)
    spread = jnp.mean((grouped - center) ** 2, axis=(1, 2), keepdims=True)
    normed = (grouped - center) * lax.rsqrt(spread + 1e-06)
    return jax.nn.silu(normed).reshape(shape)


def tap_list():
    return [(t_tap, h_tap, w_tap) for t_tap in range(3) for h_tap in range(3) for w_tap in range(3)]


def forward_shift(field, t_tap, h_tap, w_tap):
    frames, height, width = (field.shape[1], field.shape[2], field.shape[3])
    padded = jnp.pad(field, ((0, 0), (2, 0), (1, 1), (1, 1)))
    return padded[:, t_tap : t_tap + frames, h_tap : h_tap + height, w_tap : w_tap + width]


def backward_shift(field, t_tap, h_tap, w_tap):
    frames, height, width = (field.shape[1], field.shape[2], field.shape[3])
    padded = jnp.pad(field, ((0, 0), (0, 2), (1, 1), (1, 1)))
    return padded[
        :,
        2 - t_tap : 2 - t_tap + frames,
        2 - h_tap : 2 - h_tap + height,
        2 - w_tap : 2 - w_tap + width,
    ]


def conv_gathered(acts_full, kernel):
    products = jnp.einsum("cthw,okc->kothw", acts_full, kernel, preferred_element_type=jnp.float32)
    total = None
    for index, (t_tap, h_tap, w_tap) in enumerate(tap_list()):
        moved = forward_shift(products[index], t_tap, h_tap, w_tap)
        total = moved if total is None else total + moved
    return total


def spread_columns(grads):
    pieces = [backward_shift(grads, t_tap, h_tap, w_tap) for t_tap, h_tap, w_tap in tap_list()]
    return jnp.stack(pieces, axis=0)


def shards(block_in, conv_one, conv_two, out_cotangent):
    in_float = block_in[0].astype(jnp.float32)
    cotangent = out_cotangent[0]
    first_float, first_pull = jax.vjp(norm_act, in_float)
    act_one_local = first_float.astype(jnp.bfloat16)
    act_one = lax.all_gather(act_one_local, "chan", axis=0, tiled=True)
    hidden = conv_gathered(act_one, conv_one)
    second_float, second_pull = jax.vjp(norm_act, hidden)
    act_two_local = second_float.astype(jnp.bfloat16)
    act_two = lax.all_gather(act_two_local, "chan", axis=0, tiled=True)
    block_out = in_float + conv_gathered(act_two, conv_two)
    cot_columns = spread_columns(cotangent)
    two_grad = jnp.einsum(
        "cthw,kothw->okc", act_two, cot_columns, preferred_element_type=jnp.float32
    )
    partial_two = jnp.einsum(
        "kothw,okc->cthw", cot_columns, conv_two, preferred_element_type=jnp.float32
    )
    act_two_grad = lax.psum_scatter(partial_two, "chan", scatter_dimension=0, tiled=True)
    hidden_grad = second_pull(act_two_grad)[0].astype(jnp.bfloat16)
    hidden_columns = spread_columns(hidden_grad)
    one_grad = jnp.einsum(
        "cthw,kothw->okc", act_one, hidden_columns, preferred_element_type=jnp.float32
    )
    partial_one = jnp.einsum(
        "kothw,okc->cthw", hidden_columns, conv_one, preferred_element_type=jnp.float32
    )
    act_one_grad = lax.psum_scatter(partial_one, "chan", scatter_dimension=0, tiled=True)
    in_grad = cotangent.astype(jnp.float32) + first_pull(act_one_grad)[0]
    one_grad, two_grad = lax.psum((one_grad, two_grad), "clip")
    return (block_out[None], in_grad[None], one_grad, two_grad)


def solution(mesh):
    in_specs = (
        P("clip", "chan", None, None, None),
        P("chan", None, None),
        P("chan", None, None),
        P("clip", "chan", None, None, None),
    )
    out_specs = (
        P("clip", "chan", None, None, None),
        P("clip", "chan", None, None, None),
        P("chan", None, None),
        P("chan", None, None),
    )
    return jax.shard_map(shards, mesh=mesh, in_specs=in_specs, out_specs=out_specs, check_vma=False)
```

profile of v0, /device:TPU:2, one launch (start us, length us, event | category | flops | bytes accessed | tf_op | source)
XLA Modules:
  0.0 473.6 jit_solution(7996357429404227542)
XLA Ops:
  7.2 1.1 convert_reduce_fusion
  8.7 1.1 fusion.58
  10.2 1.7 fusion.47
  12.0 0.9 copy.76
  15.3 2.4 fusion.4
  17.8 2.2 copy.75
  20.1 49.3 %all-gather.3.cloned.1.call-done = bf16[512,4,4,128]{3,0,2,1:T(8,128)(2,1)} async-done(((bf16[32,4,4,128]{3,0,2,1:T(8,128)(2,1)}), bf16[512,4,4,128]{3,0,2,1:T(8,128)(2,1)}) %all-gather.3.cloned.1.call-update) | async-done | bytes 2097168 | tf_op jit(solution)/shard_map/all_gather | solution.py:60
  69.3 3.6 convolution_bitcast_fusion.1
  73.2 1.0 slice_bitcast_fusion.53
  76.1 84.6 %reduce-scatter.3.cloned.1.call-done = f32[32,4,4,128]{3,0,2,1:T(8,128)} async-done(((f32[512,4,4,128]{3,0,2,1:T(8,128)}), f32[32,4,4,128]{3,0,2,1:T(8,128)}) %reduce-scatter.3.cloned.1.call-update) | async-done | bytes 262160 | tf_op jit(solution)/shard_map/reduce_scatter | solution.py:73
  160.7 1.3 multiply_reduce_fusion.3
  166.6 2.4 fusion.7
  169.0 2.2 copy.74
  171.3 5.9 %fusion.16 = f32[32,27,512]{2,0,1:T(8,128)} fusion(bf16[27,32,4,4,128]{4,1,3,2,0:T(8,128)(2,1)} %copy-done.6, bf16[512,4,4,128]{3,0,2,1:T(8,128)(2,1)} %all-gather.3.cloned.1.call-done), kind=kOutput, calls=%fused_computation.68 | convolution fusion | flops 1811939328 | bytes 7405568 | tf_op jit(solution)/shard_map/cthw,kothw->okc/dot_general | solution.py:76
  177.2 40.5 %all-gather.5.cloned.1.call-done = bf16[512,4,4,128]{3,0,2,1:T(8,128)(2,1)} async-done(((bf16[32,4,4,128]{3,0,2,1:T(8,128)(2,1)}), bf16[512,4,4,128]{3,0,2,1:T(8,128)(2,1)}) %all-gather.5.cloned.1.call-update) | async-done | bytes 2097168 | tf_op jit(solution)/shard_map/all_gather | solution.py:64
  217.7 5.9 %fusion.19 = f32[32,27,512]{2,0,1:T(8,128)} fusion(bf16[27,32,4,4,128]{4,1,3,2,0:T(8,128)(2,1)} %copy-done.5, bf16[512,4,4,128]{3,0,2,1:T(8,128)(2,1)} %all-gather.5.cloned.1.call-done), kind=kOutput, calls=%fused_computation.69 | convolution fusion | flops 1811939328 | bytes 7405568 | tf_op jit(solution)/shard_map/cthw,kothw->okc/dot_general | solution.py:67
  223.6 3.6 convolution_bitcast_fusion
  227.4 1.0 slice_bitcast_fusion.26
  230.2 78.7 %reduce-scatter.5.cloned.1.call-done = f32[32,4,4,128]{3,0,2,1:T(8,128)} async-done(((f32[512,4,4,128]{3,0,2,1:T(8,128)}), f32[32,4,4,128]{3,0,2,1:T(8,128)}) %reduce-scatter.5.cloned.1.call-update) | async-done | bytes 262160 | tf_op jit(solution)/shard_map/reduce_scatter | solution.py:82
  308.9 1.3 fusion.219
  310.4 1.3 fusion.112
  313.6 149.2 %all-reduce.57.cloned.1.call-done = (f32[32,27,512]{2,0,1:T(8,128)}, f32[32,27,512]{2,0,1:T(8,128)}) async-done(((f32[32,27,512]{2,0,1:T(8,128)}, f32[32,27,512]{2,0,1:T(8,128)}), (f32[32,27,512]{2,0,1:T(8,128)}, f32[32,27,512]{2,0,1:T(8,128)})) %all-reduce.57.cloned.1.call-update) | async-done | bytes 3538960 | tf_op jit(solution)/shard_map/psum | solution.py:84
  462.8 3.1 copy.131
  465.9 1.2 copy.132
  (135 shorter events, 13.9 us)
Async XLA Ops:
  7.2 62.2 %copy-start = (bf16[32,27,512]{2,0,1:T(8,128)(2,1)S(1)}, bf16[32,27,512]{2,0,1:T(8,128)(2,1)}, u32[]{:S(2)}) copy-start(bf16[32,27,512]{2,0,1:T(8,128)(2,1)} %param.5) | copy-start | bytes 2654212
  7.2 7.7 %copy-start.4 = (bf16[1,32,4,4,128]{4,3,2,1,0:T(4,128)(2,1)S(1)}, bf16[1,32,4,4,128]{4,3,2,1,0:T(4,128)(2,1)}, u32[]{:S(2)}) copy-start(bf16[1,32,4,4,128]{4,3,2,1,0:T(4,128)(2,1)} %param.7) | copy-start | bytes 393220
  7.2 62.1 %all-gather.3.cloned.1.call-start = ((), (), s32[]{:S(2)}) async-start(), calls=%async_computation.2 | async-start | bytes 2228224 | tf_op jit(solution)/shard_map/all_gather | solution.py:60
  12.0 148.7 %reduce-scatter.3.cloned.1.call-start = ((), (), s32[]{:S(2)}) async-start(), calls=%async_computation.4 | async-start | bytes 4456448 | tf_op jit(solution)/shard_map/reduce_scatter | solution.py:73
  13.0 2.4 copy-start.7
  15.3 2.5 copy-start.5
  20.0 197.7 %all-gather.5.cloned.1.call-start = ((), (), s32[]{:S(2)}) async-start(), calls=%async_computation.3 | async-start | bytes 2228224 | tf_op jit(solution)/shard_map/all_gather | solution.py:64
  164.0 144.9 %reduce-scatter.5.cloned.1.call-start = ((), (), s32[]{:S(2)}) async-start(), calls=%async_computation.5 | async-start | bytes 4456448 | tf_op jit(solution)/shard_map/reduce_scatter | solution.py:82
  166.6 2.5 copy-start.6
  171.3 291.5 %all-reduce.57.cloned.1.call-start = ((), (), s32[]{:S(2)}) async-start(), calls=%async_computation.6 | async-start | bytes 7077888 | tf_op jit(solution)/shard_map/psum | solution.py:84
  227.4 1.0 copy-start.2
  462.8 3.1 copy-start.3
  462.8 4.3 copy-start.1
Sparse Core Ops, SparseCore 0:
  12.1 57.1 all-gather.2
  73.7 86.9 reduce-scatter.2
  164.2 53.5 all-gather.4
  221.9 86.9 reduce-scatter.4
  312.0 150.6 all-reduce.56
where the time goes:
time: 474 us
  waiting for transfers between devices  402 us (85%)
  matrix products  23.8 us (5%)
  local copies, waits for them, and re-layouts  20.3 us (4%)
  between operations  14.2 us (3%)
  other arithmetic  12.5 us (3%)
    psum x1, waiting for transfers between devices, shards(): one_grad, two_grad = lax.psum((one_grad, two_grad), 'clip')  149 us
    reduce_scatter x1, waiting for transfers between devices, shards(): lax.psum_scatter(partial_two, 'chan', scatter_dimension=0, tiled=True)  84.6 us
    reduce_scatter x1, waiting for transfers between devices, shards(): lax.psum_scatter(partial_one, 'chan', scatter_dimension=0, tiled=True)  78.7 us
    all_gather x1, waiting for transfers between devices, shards(): act_one = lax.all_gather(act_one_local, 'chan', axis=0, tiled=True)  49.3 us
    all_gather x1, waiting for transfers between devices, shards(): act_two = lax.all_gather(act_two_local, 'chan', axis=0, tiled=True)  40.5 us
    unnamed x73, local copies, waits for them, and re-layouts  11.2 us
  transfers between devices with their start and end apart: 5, of which 5 were waited for; matrix products, arithmetic and copies ran while one was open for 9% of the time, Pallas kernels for 0%

commit v1 on v0

--- a/solution.py
+++ b/solution.py
@@ -2,6 +2,7 @@
 import jax.numpy as jnp
 from jax import lax
 from jax.sharding import PartitionSpec as P
+from jax.lax import all_to_all, axis_size
 
 C = 512
 GROUPS = 32
@@ -53,11 +54,19 @@
 
 
 def shards(block_in, conv_one, conv_two, out_cotangent):
+
+    def state_group(original):
+        f_now = all_to_all(
+            jnp.stack([original] * axis_size("chan")), axis_name="chan", split_axis=0, concat_axis=0
+        )
+        frame_out = jnp.concatenate(f_now, axis=0)
+        return frame_out
+
     in_float = block_in[0].astype(jnp.float32)
     cotangent = out_cotangent[0]
     first_float, first_pull = jax.vjp(norm_act, in_float)
     act_one_local = first_float.astype(jnp.bfloat16)
-    act_one = lax.all_gather(act_one_local, "chan", axis=0, tiled=True)
+    act_one = state_group(act_one_local)
     hidden = conv_gathered(act_one, conv_one)
     second_float, second_pull = jax.vjp(norm_act, hidden)
     act_two_local = second_float.astype(jnp.bfloat16)

time: 474 us -> 421 us (0.89)
  waiting for transfers between devices: 402 us -> 318 us
  blocking collectives: 0 us -> 34.1 us
    all_gather x1 -> x0, waiting for transfers between devices: 49.3 us -> none  [shards(): act_one = lax.all_gather(act_one_local, 'chan', axis=0, tiled=True)]
    reduce_scatter x1, waiting for transfers between devices: 84.6 us -> 48.9 us  [shards(): lax.psum_scatter(partial_two, 'chan', scatter_dimension=0, tiled=True)]
    all_to_all x0 -> x1, blocking collectives: none -> 34.1 us  [state_group(): all_to_all(jnp.stack([original] * axis_size('chan')), axis_name='chan', s...]
    unnamed x73 -> x79, local copies, waits for them, and re-layouts: 11.2 us -> 13.8 us
  transfers between devices with their start and end apart: 5 -> 4, of which waited for: 5 -> 4; matrix products, arithmetic and copies ran while one was open for 9% -> 8% of each run, Pallas kernels for 0% -> 0%
where the time goes in v1:
time: 421 us
  waiting for transfers between devices  318 us (76%)
  blocking collectives  34.1 us (8%)
  local copies, waits for them, and re-layouts  23.8 us (6%)
  matrix products  20 us (5%)
  between operations  14.2 us (3%)
  other arithmetic  10.6 us (3%)
    psum x1, waiting for transfers between devices, shards(): one_grad, two_grad = lax.psum((one_grad, two_grad), 'clip')  149 us
    reduce_scatter x1, waiting for transfers between devices, shards(): lax.psum_scatter(partial_one, 'chan', scatter_dimension=0, tiled=True)  78.7 us
    reduce_scatter x1, waiting for transfers between devices, shards(): lax.psum_scatter(partial_two, 'chan', scatter_dimension=0, tiled=True)  48.9 us
    all_gather x1, waiting for transfers between devices, shards(): act_two = lax.all_gather(act_two_local, 'chan', axis=0, tiled=True)  41.1 us
    all_to_all x1, blocking collectives, state_group(): all_to_all(jnp.stack([original] * axis_size('chan')), axis_name='chan', s...  34.1 us
    unnamed x79, local copies, waits for them, and re-layouts  13.8 us
  transfers between devices with their start and end apart: 4, of which 4 were waited for; matrix products, arithmetic and copies ran while one was open for 8% of the time, Pallas kernels for 0%

profile of v1, /device:TPU:2, one launch (start us, length us, event | category | flops | bytes accessed | tf_op | source)
XLA Modules:
  0.0 421.1 jit_solution(7555188195193376660)
XLA Ops:
  7.2 1.0 copy.168
  10.6 2.4 fusion.4
  13.1 2.2 copy.167
  18.0 34.1 %all_to_all.5 = bf16[16,32,4,4,128]{4,1,3,2,0:T(8,128)(2,1)S(1)} all-to-all(bf16[16,32,4,4,128]{4,1,3,2,0:T(8,128)(2,1)S(1)} %stack.188), channel_id=1, replica_groups=mesh['clip'=16,'chan'=16] {'chan'}, dimensions={0} | all-to-all | bytes 4194304 | tf_op jit(solution)/shard_map/all_to_all | solution.py:59
  52.6 2.0 convolution_bitcast_fusion.1
  55.7 0.9 fusion.217
  57.6 48.9 %reduce-scatter.3.cloned.1.call-done = f32[32,4,4,128]{3,0,2,1:T(8,128)} async-done(((f32[512,4,4,128]{3,0,2,1:T(8,128)}), f32[32,4,4,128]{3,0,2,1:T(8,128)}) %reduce-scatter.3.cloned.1.call-update) | async-done | bytes 262160 | tf_op jit(solution)/shard_map/reduce_scatter | solution.py:82
  106.5 2.0 multiply_reduce_fusion.3
  109.6 1.8 add_convert_fusion
  114.0 2.4 fusion.7
  116.5 2.2 copy.166
  118.7 5.2 %convolution_bitcast_fusion.2 = f32[32,27,512]{2,0,1:T(8,128)} fusion(bf16[27,32,4,4,128]{4,1,3,2,0:T(8,128)(2,1)} %copy-done.7, bf16[512,4,4,128,1]{3,0,2,1,4:T(8,128)(2,1)S(1)} %bitcast.535), kind=kOutput, calls=%fused_computation.66 | convolution fusion | flops 1811939328 | bytes 7405568 | tf_op jit(solution)/shard_map/cthw,kothw->okc/dot_general | solution.py:85
  124.0 41.1 %all-gather.2.cloned.1.call-done = bf16[512,4,4,128]{3,0,2,1:T(8,128)(2,1)} async-done(((bf16[32,4,4,128]{3,0,2,1:T(8,128)(2,1)}), bf16[512,4,4,128]{3,0,2,1:T(8,128)(2,1)}) %all-gather.2.cloned.1.call-update) | async-done | bytes 2097168 | tf_op jit(solution)/shard_map/all_gather | solution.py:73
  165.1 5.9 %fusion.13 = f32[32,27,512]{2,0,1:T(8,128)} fusion(bf16[27,32,4,4,128]{4,1,3,2,0:T(8,128)(2,1)} %copy-done.6, bf16[512,4,4,128]{3,0,2,1:T(8,128)(2,1)} %all-gather.2.cloned.1.call-done), kind=kOutput, calls=%fused_computation.65 | convolution fusion | flops 1811939328 | bytes 7405568 | tf_op jit(solution)/shard_map/cthw,kothw->okc/dot_general | solution.py:76
  171.0 1.6 copy-done.8
  172.8 2.0 convolution_bitcast_fusion
  175.0 1.0 slice_bitcast_fusion.26
  176.9 0.9 copy.87
  177.7 78.7 %reduce-scatter.5.cloned.1.call-done = f32[32,4,4,128]{3,0,2,1:T(8,128)} async-done(((f32[512,4,4,128]{3,0,2,1:T(8,128)}), f32[32,4,4,128]{3,0,2,1:T(8,128)}) %reduce-scatter.5.cloned.1.call-update) | async-done | bytes 262160 | tf_op jit(solution)/shard_map/reduce_scatter | solution.py:91
  256.5 1.3 fusion.214
  257.9 1.3 fusion.106
  261.2 149.1 %all-reduce.57.cloned.1.call-done = (f32[32,27,512]{2,0,1:T(8,128)}, f32[32,27,512]{2,0,1:T(8,128)}) async-done(((f32[32,27,512]{2,0,1:T(8,128)}, f32[32,27,512]{2,0,1:T(8,128)}), (f32[32,27,512]{2,0,1:T(8,128)}, f32[32,27,512]{2,0,1:T(8,128)})) %all-reduce.57.cloned.1.call-update) | async-done | bytes 3538960 | tf_op jit(solution)/shard_map/psum | solution.py:93
  410.3 3.1 copy.223
  413.4 1.2 copy.224
  (141 shorter events, 14.4 us)
Async XLA Ops:
  7.2 45.4 %copy-start = (bf16[32,27,512]{2,0,1:T(8,128)(2,1)S(1)}, bf16[32,27,512]{2,0,1:T(8,128)(2,1)}, u32[]{:S(2)}) copy-start(bf16[32,27,512]{2,0,1:T(8,128)(2,1)} %param.5) | copy-start | bytes 2654212
  7.2 3.0 copy-start.4
  7.2 99.3 %reduce-scatter.3.cloned.1.call-start = ((), (), s32[]{:S(2)}) async-start(), calls=%async_computation.4 | async-start | bytes 4456448 | tf_op jit(solution)/shard_map/reduce_scatter | solution.py:82
  8.3 2.4 copy-start.9
  10.6 2.5 copy-start.6
  15.3 0.9 copy-start.2
  15.3 149.8 %all-gather.2.cloned.1.call-start = ((), (), s32[]{:S(2)}) async-start(), calls=%async_computation.3 | async-start | bytes 2228224 | tf_op jit(solution)/shard_map/all_gather | solution.py:73
  111.5 145.0 %reduce-scatter.5.cloned.1.call-start = ((), (), s32[]{:S(2)}) async-start(), calls=%async_computation.5 | async-start | bytes 4456448 | tf_op jit(solution)/shard_map/reduce_scatter | solution.py:91
  114.0 2.5 copy-start.7
  118.7 291.6 %all-reduce.57.cloned.1.call-start = ((), (), s32[]{:S(2)}) async-start(), calls=%async_computation.6 | async-start | bytes 7077888 | tf_op jit(solution)/shard_map/psum | solution.py:93
  171.0 1.6 copy-start.8
  171.0 1.8 copy-start.10
  176.0 84.1 %copy-start.5 = (bf16[1,32,4,4,128]{4,3,2,1,0:T(4,128)(2,1)S(1)}, bf16[1,32,4,4,128]{4,3,2,1,0:T(4,128)(2,1)}, u32[]{:S(2)}) copy-start(bf16[1,32,4,4,128]{4,3,2,1,0:T(4,128)(2,1)} %param.7) | copy-start | bytes 393220
  410.3 3.1 copy-start.3
  410.3 4.3 %copy-start.1 = (bf16[32,27,512]{2,0,1:T(8,128)(2,1)S(1)}, bf16[32,27,512]{2,0,1:T(8,128)(2,1)}, u32[]{:S(2)}) copy-start(bf16[32,27,512]{2,0,1:T(8,128)(2,1)} %param.5) | copy-start | bytes 2654212
Sparse Core Ops, SparseCore 0:
  15.5 90.9 reduce-scatter.2
  111.6 53.4 all-gather.1
  169.5 86.9 reduce-scatter.4
  259.6 150.6 all-reduce.56
